TPU v7x, 32 devices: a whole 2x2x4 slice. The times are simulated.
32 devices in a mesh: wide: 8 (over y, x, core), narrow: 4 (over z).
Axes of the slice: x: 2, y: 2, z: 4, core: 2. Of those that a mesh axis runs over, the one named last changes fastest.
Arguments:
- reference_image: bfloat16 [1024, 512, 128], P('wide', 'narrow'), may hold values from -6 to 6
- deformed_image: bfloat16 [1024, 512, 128], P('wide', 'narrow'), may hold values from -6 to 6
- displacement: float32 [3, 17, 128, 64], P(None, None, 'wide', 'narrow'), may hold values from -0.5 to 0.5
- tile_map: int32 [8, 4, 2], P('wide', 'narrow'), may hold values from -32 to 32, as said below
Outputs:
- updated: float32 [3, 17, 128, 64], P(None, None, 'wide', 'narrow')
- residual: bfloat16 [1024, 512, 128], P('wide', 'narrow')
Inputs may be any that keep to these rules, and one draw needn't show every extreme that they name: `tile_map`: each component spans -32 to 32 over the tiles and reaches both ends on some tile.
All inputs are finite; a program needn't handle non-finite values.
Results may differ from a plain program's by a relative error of at most 0.0004.
Values may be sent and summed in bfloat16 or wider, within the bound.
A program may use at most 256 MiB of HBM per device.

v0:
```python
import functools

import jax
import jax.numpy as jnp
import numpy as np
from jax import lax
from jax.experimental import pallas as pl
from jax.experimental.pallas import tpu as pltpu
from jax.sharding import PartitionSpec as P

MU_SHEAR = 1.0
LAMBDA_BULK = 2.0
REG_WEIGHT = 256.0
STIFFNESS = 16.0
MESH = pl.DeviceIdType.MESH
F32 = jnp.float32
BF16 = jnp.bfloat16
SIDE = 48
QPAD = 24


def shifted(array, axis, by):
    size = lax.axis_size(axis)
    pairs = [(i, i + by) for i in range(size) if 0 <= i + by < size]
    return lax.ppermute(array, axis, pairs)


def halo_kernel(nw, nn, rim, own, ext, zeros, send, recv, zsem, lsem):
    rows, cols, _ = own.shape
    w = lax.axis_index("wide")
    n = lax.axis_index("narrow")
    lo_w, hi_w, lo_n, hi_n = w > 0, w < nw - 1, n > 0, n < nn - 1
    up_w, dn_w = (w + 1, n), (w - 1, n)
    up_n, dn_n = (w, n + 1), (w, n - 1)
    mid = slice(SIDE, SIDE + cols)
    ylo = slice(0, SIDE)
    yhi = slice(SIDE + cols, SIDE + cols + SIDE)
    barrier = pltpu.get_barrier_semaphore()
    sides = ((lo_w, dn_w), (hi_w, up_w), (lo_n, dn_n), (hi_n, up_n))
    for there, device in sides:
        @pl.when(there)
        def _(device=device):
            pl.semaphore_signal(barrier, inc=1, device_id=device, device_id_type=MESH)
    zeros[...] = jnp.zeros_like(zeros)
    as_int = lambda flag: flag.astype(jnp.int32)
    pl.semaphore_wait(barrier, as_int(lo_w) + as_int(hi_w) + as_int(lo_n) + as_int(hi_n))

    def remote(k, src, dst, device):
        return pltpu.make_async_remote_copy(
            src_ref=src, dst_ref=dst, send_sem=send.at[k], recv_sem=recv.at[k],
            device_id=device, device_id_type=MESH)

    full = (slice(0, rim), slice(rim, rows - rim), slice(rows - rim, rows))
    copies = []
    for j in (0, 2, 1):
        part = full[j]
        there = slice(part.start + rim, part.stop + rim)
        copies.append((hi_n, lo_n, remote(j, own.at[part, cols - SIDE:cols], ext.at[there, ylo], up_n)))
        copies.append((lo_n, hi_n, remote(3 + j, own.at[part, 0:SIDE], ext.at[there, yhi], dn_n)))
    copies.append((hi_w, lo_w, remote(6, own.at[rows - rim:rows], ext.at[0:rim, mid], up_w)))
    copies.append((lo_w, hi_w, remote(7, own.at[0:rim], ext.at[rows + rim:rows + 2 * rim, mid], dn_w)))
    for goes, _c, copy in copies:
        @pl.when(goes)
        def _(copy=copy):
            copy.start()
    local = pltpu.make_async_copy(own, ext.at[rim:rim + rows, mid], lsem)
    local.start()
    total = rows + 2 * rim

    def fills():
        out = []
        out.append((jnp.logical_not(lo_n), 0, zeros.at[:, 0:SIDE], ext.at[:, ylo]))
        out.append((jnp.logical_not(hi_n), 1, zeros.at[:, 0:SIDE], ext.at[:, yhi]))
        out.append((jnp.logical_not(lo_w), 2, None, slice(0, rim)))
        out.append((jnp.logical_not(hi_w), 3, None, slice(rim + rows, total)))
        return out

    jobs = []
    for cond, k, src, dst in fills()[:2]:
        jobs.append((cond, pltpu.make_async_copy(src, dst, zsem.at[k])))
    for k, (cond, band) in enumerate(((jnp.logical_not(lo_w), slice(0, rim)), (jnp.logical_not(hi_w), slice(rim + rows, total)))):
        jobs.append((cond, pltpu.make_async_copy(zeros.at[0:rim, 0:cols], ext.at[band, mid], zsem.at[2 + k])))
        jobs.append((cond & lo_n, pltpu.make_async_copy(zeros.at[0:rim, 0:SIDE], ext.at[band, ylo], zsem.at[4 + k])))
        jobs.append((cond & hi_n, pltpu.make_async_copy(zeros.at[0:rim, 0:SIDE], ext.at[band, yhi], zsem.at[6 + k])))
    for cond, job in jobs:
        @pl.when(cond)
        def _(job=job):
            job.start()
    corners = []
    low_rows, high_rows = slice(rim, 2 * rim), slice(rows, rows + rim)
    below, above = slice(0, rim), slice(rim + rows, total)
    corners.append((lo_n & lo_w, lo_n & hi_w, remote(8, ext.at[low_rows, ylo], ext.at[above, ylo], dn_w)))
    corners.append((hi_n & lo_w, hi_n & hi_w, remote(9, ext.at[low_rows, yhi], ext.at[above, yhi], dn_w)))
    corners.append((lo_n & hi_w, lo_n & lo_w, remote(10, ext.at[high_rows, ylo], ext.at[below, ylo], up_w)))
    corners.append((hi_n & hi_w, hi_n & lo_w, remote(11, ext.at[high_rows, yhi], ext.at[below, yhi], up_w)))
    for (_g, comes, copy), corner in zip(copies[:4], corners):
        @pl.when(comes)
        def _(copy=copy):
            copy.wait_recv()
        @pl.when(corner[0])
        def _(corner=corner):
            corner[2].start()
    for _g, comes, copy in copies[4:] + corners:
        @pl.when(comes)
        def _(copy=copy):
            copy.wait_recv()
    for goes, _c, copy in copies + corners:
        @pl.when(goes)
        def _(copy=copy):
            copy.wait_send()
    for cond, job in jobs:
        @pl.when(cond)
        def _(job=job):
            job.wait()
    local.wait()


def exchange(deformed, nw, nn):
    rows, cols, layers = deformed.shape
    rim = rows // 4 + 1
    shape = (rows + 2 * rim, cols + 2 * SIDE, layers)
    return pl.pallas_call(
        functools.partial(halo_kernel, nw, nn, rim),
        out_shape=jax.ShapeDtypeStruct(shape, BF16),
        in_specs=[pl.BlockSpec(memory_space=pl.ANY)],
        out_specs=pl.BlockSpec(memory_space=pl.ANY),
        scratch_shapes=[
            pltpu.VMEM((shape[0], cols, layers), BF16),
            pltpu.SemaphoreType.DMA((12,)),
            pltpu.SemaphoreType.DMA((12,)),
            pltpu.SemaphoreType.DMA((8,)),
            pltpu.SemaphoreType.DMA,
        ],
        compiler_params=pltpu.CompilerParams(
            collective_id=0, has_side_effects=True, vmem_limit_bytes=32 << 20),
        name="halo",
    )(deformed)


def tables(rows, cols, layers, comps):
    def one(voxels):
        t = np.zeros((voxels, voxels // 8 + 1))
        for i in range(voxels):
            f = (i % 8 + 0.5) / 8.0
            t[i, i // 8] += 1.0 - f
            t[i, i // 8 + 1] += f
        return t
    ty, tz = one(cols), one(layers)
    nq, ns = ty.shape[1], tz.shape[1]
    typ = np.zeros((cols, QPAD))
    typ[:, :nq] = ty
    frac = (np.arange(8) + 0.5) / 8.0
    wx = np.stack([1.0 - frac, frac], 1)
    inter = 0.5 * np.einsum("ka,yq->kyaq", wx, typ)
    inter = np.concatenate([inter[:, :, 0], inter[:, :, 0], inter[:, :, 1], inter[:, :, 1]], -1)
    inter = inter.reshape(8 * cols, 4 * QPAD)
    proj = np.concatenate([typ.T, typ.T], 1)
    diag = np.einsum("ka,yq->aqky", wx * wx, typ * typ).reshape(2 * QPAD, 8 * cols)
    dhi = diag.astype(BF16).astype(np.float64)
    diag = np.concatenate([dhi, diag - dhi], 0)
    lanes = comps * layers
    up = np.zeros((2 * comps * ns, lanes))
    down = np.zeros((lanes, 128))
    down2 = np.zeros((lanes, 128))
    for c in range(comps):
        for h in range(2):
            up[(h * comps + c) * ns:(h * comps + c + 1) * ns, c * layers:(c + 1) * layers] = tz.T
        down[c * layers:(c + 1) * layers, c * ns:(c + 1) * ns] = -0.5 * tz
        down2[c * layers:(c + 1) * layers, c * ns:(c + 1) * ns] = 0.25 * tz * tz
    dz = np.zeros((layers, layers))
    for z in range(layers):
        if z + 1 < layers:
            dz[z + 1, z] = 1.0
        if z > 0:
            dz[z - 1, z] = -1.0
    as_bf16 = lambda a: jnp.asarray(a.astype(BF16))
    return [as_bf16(a) for a in (inter, proj, diag, up, down, down2, dz)]


def split(value):
    high = value.astype(BF16)
    return high, (value - high.astype(F32)).astype(BF16)


def tile_kernel(rim, map_ref, ref_tile, ext, nodes, inter, proj, diag, up, down, down2, dz,
                res, grad_out, diag_out,
                rows_in, shift, samp, ndz, moved, gy, gz, sums, sq, gacc, dacc, sem):
    p = pl.program_id(0)
    steps = pl.num_programs(0)
    cols, layers = samp.shape[1], samp.shape[2]
    comps = ndz.shape[2] // layers
    start = map_ref[0] + (rim - 1)

    def fetch(first, count, k):
        return pltpu.make_async_copy(
            ext.at[pl.ds(start + first, count)], rows_in.at[pl.ds(first, count)], sem.at[k])

    def sample(first, count):
        for a in range(0, count, 2):
            pair = jnp.concatenate([rows_in[first + a], rows_in[first + a + 1]], axis=1)
            got = jnp.dot(shift[...], pair, preferred_element_type=F32)
            for b in range(2):
                samp[first + a + b] = got[:cols, b * layers:(b + 1) * layers]
                gy[(first + a + b) % 16] = got[cols:, b * layers:(b + 1) * layers]

    @pl.when(p == 0)
    def _():
        fetch(0, 2, steps).start()

        @pl.loop(0, steps)
        def _(k):
            fetch(8 * k + 2, 8, k).start()
        y = lax.broadcasted_iota(jnp.int32, (cols, shift.shape[1]), 0)
        k = lax.broadcasted_iota(jnp.int32, (cols, shift.shape[1]), 1)
        gap = k - y - (map_ref[1] + SIDE)
        shift[:cols] = jnp.where(gap == 0, 1.0, 0.0).astype(BF16)
        shift[cols:] = (jnp.where(gap == 1, 1.0, 0.0) - jnp.where(gap == -1, 1.0, 0.0)).astype(BF16)
        high = nodes[...].astype(BF16).astype(F32)
        both = jnp.concatenate([high, nodes[...] - high], axis=1).astype(BF16)
        level = jnp.dot(both, up[...], preferred_element_type=F32)
        for i in range(ndz.shape[0]):
            part = level[i * QPAD:(i + 1) * QPAD]
            head = part.astype(BF16).astype(F32)
            ndz[i] = jnp.concatenate([head, part - head], axis=0).astype(BF16)
        gacc[...] = jnp.zeros_like(gacc)
        dacc[...] = jnp.zeros_like(dacc)
        fetch(0, 2, steps).wait()
        sample(0, 2)

    base = pl.multiple_of(8 * p, 8)
    fetch(base + 2, 8, p).wait()
    sample(base + 2, 8)
    gz[...] = jnp.dot(samp[pl.ds(base + 1, 8)].reshape(8 * cols, layers).astype(BF16), dz[...],
                      preferred_element_type=F32)
    level = ndz[pl.ds(p, 2)].reshape(4 * QPAD, comps * layers)
    moved[...] = jnp.dot(inter[...], level, preferred_element_type=F32)

    chunk = 32

    @pl.loop(0, cols // chunk)
    def _(j):
        at = pl.multiple_of(j * chunk, chunk)
        span = pl.ds(at, chunk)
        run = [None] * comps
        tot = [None] * comps
        for k in range(8):
            line = pl.ds(k * cols + at, chunk)
            here = samp[base + 1 + k, span, :]
            g = [samp[base + 2 + k, span, :] - samp[base + k, span, :],
                 gy[(base + 1 + k) % 16, span, :],
                 gz[line, :]]
            r = ref_tile[k, span, :].astype(F32) - here
            for c in range(3):
                r = r - g[c] * moved[line, c * layers:(c + 1) * layers]
            res[k, span, :] = r.astype(BF16)
            for c in range(3):
                f = g[c] * r
                run[c] = f if k == 0 else run[c] + f
                tot[c] = run[c] if k == 0 else tot[c] + run[c]
                sq[line, c * layers:(c + 1) * layers] = (g[c] * g[c]).astype(BF16)
        for c in range(3):
            low = (tot[c] - 0.5 * run[c]) * 0.125
            for a, value in enumerate((low, run[c] - low)):
                head, tail = split(value)
                sums[a, span, c * layers:(c + 1) * layers] = head
                sums[a, pl.ds(cols + at, chunk), c * layers:(c + 1) * layers] = tail

    for a in range(2):
        gacc[p + a] = gacc[p + a] + jnp.dot(proj[...], sums[a], preferred_element_type=F32)
    got = jnp.dot(diag[...], sq[...], preferred_element_type=F32)
    for a in range(2):
        dacc[p + a] = dacc[p + a] + (got[a * QPAD:(a + 1) * QPAD] + got[(2 + a) * QPAD:(3 + a) * QPAD])

    @pl.when(p == steps - 1)
    def _():
        for acc, table, out in ((gacc, down, grad_out), (dacc, down2, diag_out)):
            flat = acc[...].reshape(-1, comps * layers)
            head, tail = split(flat)
            out[...] = (jnp.dot(head, table[...], preferred_element_type=F32)
                        + jnp.dot(tail, table[...], preferred_element_type=F32))


def tile_terms(reference_tile, ext, nodal_field, offsets):
    rows, cols, layers = reference_tile.shape
    comps, ns, npx, nq = nodal_field.shape
    rim = rows // 4 + 1
    tabs = tables(rows, cols, layers, comps)
    nodes = jnp.pad(nodal_field.transpose(2, 3, 0, 1), ((0, 0), (0, QPAD - nq), (0, 0), (0, 0)))
    nodes = nodes.reshape(npx * QPAD, comps * ns)
    steps = rows // 8
    whole = lambda a: pl.BlockSpec(a.shape, lambda p, m: (0,) * a.ndim, pipeline_mode=pl.Buffered(1))
    slab = pl.BlockSpec((8, cols, layers), lambda p, m: (p, 0, 0))
    out_nodes = jax.ShapeDtypeStruct((npx * QPAD, 128), F32)
    grid_spec = pltpu.PrefetchScalarGridSpec(
        num_scalar_prefetch=1,
        grid=(steps,),
        in_specs=[slab, pl.BlockSpec(memory_space=pl.ANY), whole(nodes)] + [whole(t) for t in tabs],
        out_specs=[slab, whole(out_nodes), whole(out_nodes)],
        scratch_shapes=[
            pltpu.VMEM((rows + 2, cols + 2 * SIDE, layers), BF16),
            pltpu.VMEM((2 * cols, cols + 2 * SIDE), BF16),
            pltpu.VMEM((rows + 2, cols, layers), F32),
            pltpu.VMEM((npx, 2 * QPAD, comps * layers), BF16),
            pltpu.VMEM((8 * cols, comps * layers), F32),
            pltpu.VMEM((16, cols, layers), F32),
            pltpu.VMEM((8 * cols, layers), F32),
            pltpu.VMEM((2, 2 * cols, comps * layers), BF16),
            pltpu.VMEM((8 * cols, comps * layers), BF16),
            pltpu.VMEM((npx, QPAD, comps * layers), F32),
            pltpu.VMEM((npx, QPAD, comps * layers), F32),
            pltpu.SemaphoreType.DMA((steps + 1,)),
        ],
    )
    res, grad, diag = pl.pallas_call(
        functools.partial(tile_kernel, rim),
        grid_spec=grid_spec,
        out_shape=[jax.ShapeDtypeStruct(reference_tile.shape, BF16), out_nodes, out_nodes],
        compiler_params=pltpu.CompilerParams(
            dimension_semantics=("arbitrary",), vmem_limit_bytes=56 << 20),
        name="tile",
    )(offsets, reference_tile, ext, nodes, *tabs)
    back = lambda a: a.reshape(npx, QPAD, 128)[:, :nq, :comps * ns].reshape(npx, nq, comps, ns).transpose(2, 3, 0, 1)
    return res, back(grad), back(diag)


def element_energy(nodal_field):
    diff_x = nodal_field[:, :, 1:, :] - nodal_field[:, :, :-1, :]
    grad_x = 0.03125 * (
        diff_x[:, :-1, :, :-1]
        + diff_x[:, 1:, :, :-1]
        + diff_x[:, :-1, :, 1:]
        + diff_x[:, 1:, :, 1:]
    )
    diff_y = nodal_field[:, :, :, 1:] - nodal_field[:, :, :, :-1]
    grad_y = 0.03125 * (
        diff_y[:, :-1, :-1, :]
        + diff_y[:, 1:, :-1, :]
        + diff_y[:, :-1, 1:, :]
        + diff_y[:, 1:, 1:, :]
    )
    diff_z = nodal_field[:, 1:, :, :] - nodal_field[:, :-1, :, :]
    grad_z = 0.03125 * (
        diff_z[:, :, :-1, :-1]
        + diff_z[:, :, 1:, :-1]
        + diff_z[:, :, :-1, 1:]
        + diff_z[:, :, 1:, 1:]
    )
    columns = (grad_x, grad_y, grad_z)
    entries = [[columns[j][i] + (1.0 if i == j else 0.0) for j in range(3)] for i in range(3)]
    volume_ratio = (
        entries[0][0] * (entries[1][1] * entries[2][2] - entries[1][2] * entries[2][1])
        - entries[0][1] * (entries[1][0] * entries[2][2] - entries[1][2] * entries[2][0])
        + entries[0][2] * (entries[1][0] * entries[2][1] - entries[1][1] * entries[2][0])
    )
    squares = entries[0][0] * entries[0][0]
    for i in range(3):
        for j in range(3):
            if i + j > 0:
                squares = squares + entries[i][j] * entries[i][j]
    log_ratio = jnp.log(volume_ratio)
    energy = (
        0.5 * MU_SHEAR * (squares - 3.0 - 2.0 * log_ratio)
        + 0.5 * LAMBDA_BULK * log_ratio * log_ratio
    )
    return REG_WEIGHT * jnp.sum(energy)


def per_device(nw, nn, reference_image, deformed_image, displacement, tile_map):
    from_next = shifted(displacement[:, :, 0, :], "wide", -1)
    nodal_wide = jnp.concatenate([displacement, from_next[:, :, None, :]], axis=2)
    from_above = shifted(nodal_wide[:, :, :, 0], "narrow", -1)
    nodal_field = jnp.concatenate([nodal_wide, from_above[:, :, :, None]], axis=3)
    energy_value, energy_pull = jax.vjp(element_energy, nodal_field)
    reg_grad = energy_pull(jnp.ones_like(energy_value))[0]
    ext = exchange(deformed_image, nw, nn)
    residual, data_grad, data_diag = tile_terms(
        reference_image, ext, nodal_field, tile_map.reshape(2))
    both = jnp.stack([data_grad + reg_grad, data_diag])
    got_wide = shifted(both[:, :, :, -1, :], "wide", 1)
    both = both[:, :, :, :-1, :].at[:, :, :, 0, :].add(got_wide)
    got_narrow = shifted(both[:, :, :, :, -1], "narrow", 1)
    both = both[:, :, :, :, :-1].at[:, :, :, :, 0].add(got_narrow)
    updated = displacement - both[0] / (both[1] + STIFFNESS)
    return (updated, residual)


def solution(mesh):
    placed = (
        P("wide", "narrow", None),
        P("wide", "narrow", None),
        P(None, None, "wide", "narrow"),
        P("wide", "narrow", None),
    )
    return jax.shard_map(
        functools.partial(per_device, mesh.shape["wide"], mesh.shape["narrow"]),
        mesh=mesh,
        in_specs=placed,
        out_specs=(P(None, None, "wide", "narrow"), P("wide", "narrow", None)),
        check_vma=False,
    )
```

profile of v0, /device:TPU:12, one launch (start us, length us, event | category | flops | bytes accessed | tf_op | source)
XLA Modules:
  0.0 120.7 jit_solution(7300133319143494236)
XLA Ops:
  0.6 0.7 slice_bitcast_fusion
  1.4 2.8 %collective-permute-start = (f32[3,17,16]{1,2,0:T(8,128)S(1)}, f32[3,17,16]{1,2,0:T(8,128)S(1)}, u32[]{:S(2)}, u32[]{:S(2)}) collective-permute-start(f32[3,17,16]{1,2,0:T(8,128)S(1)} %slice_bitcast_fusion), channel_id=1, source_target_pairs={{4,0},{8,4},{12,8},{16,12},{20,16},{24,20},{28,24},{5,1},{9,5},{13... | collective-permute-start | bytes 9800 | tf_op jit(solution)/shard_map/ppermute | solution.py:25
  4.2 1.4 %copy.44 = f32[3,17,16,16]{2,1,0,3:T(8,128)S(1)} copy(f32[3,17,16,16]{1,3,2,0:T(8,128)} %param.17) | data formatting | bytes 104448 | tf_op args[2]
  5.5 0.1 collective-permute-done
  5.7 0.4 copy.45
  6.1 0.1 fusion.9
  6.1 2.4 %collective-permute-start.1 = (f32[3,17,17]{2,1,0:T(8,128)S(1)}, f32[3,17,17]{2,1,0:T(8,128)S(1)}, u32[]{:S(2)}, u32[]{:S(2)}) collective-permute-start(f32[3,17,17]{2,1,0:T(8,128)S(1)} %fusion.9), channel_id=1, source_target_pairs={{1,0},{2,1},{3,2},{5,4},{6,5},{7,6},{9,8},{10,9},{11,10},{13,12},{... | collective-permute-start | bytes 10412 | tf_op jit(solution)/shard_map/ppermute | solution.py:25
  8.5 0.0 copy-start.1
  8.5 2.2 %copy-done.1 = bf16[128,128,128]{2,1,0:T(8,128)(2,1)S(1)} copy-done((bf16[128,128,128]{2,1,0:T(8,128)(2,1)S(1)}, bf16[128,128,128]{2,1,0:T(8,128)(2,1)}, u32[]{:S(2)}) %copy-start.1) | copy-done | bytes 4194328
  10.7 45.2 %halo.1.ext = bf16[194,224,128]{2,1,0:T(8,128)(2,1)S(1)} custom-call(bf16[128,128,128]{2,1,0:T(8,128)(2,1)S(1)} %copy-done.1), custom_call_target="tpu_custom_call" | custom-call | tf_op jit(solution)/shard_map/halo/pallas_call | solution.py:122
  55.9 0.0 copy-start
  55.9 4.2 %copy-done = bf16[194,224,128]{2,1,0:T(8,128)(2,1)} copy-done((bf16[194,224,128]{2,1,0:T(8,128)(2,1)}, bf16[194,224,128]{2,1,0:T(8,128)(2,1)S(1)}, u32[]{:S(2)}) %copy-start) | copy-done | bytes 11124760
  60.1 0.0 collective-permute-done.1
  60.1 0.2 fusion.14
  60.3 0.2 pad_maximum_fusion
  60.5 0.2 slice_subtract_fusion.1
  60.8 0.2 slice_subtract_fusion
  61.0 0.5 copy.59
  61.6 0.2 pad.89.clone
  61.8 1.0 reshape.116.nodes
  62.8 30.4 %tile.1 = (bf16[128,128,128]{2,1,0:T(8,128)(2,1)}, f32[408,128]{1,0:T(8,128)}, f32[408,128]{1,0:T(8,128)}) custom-call(s32[2]{0:T(128)} %bitcast.46, bf16[128,128,128]{2,1,0:T(8,128)(2,1)} %ref_tile.1, bf16[194,224,128]{2,1,0:T(8,128)(2,1)} %copy-done, f32[408,51]{1,0:T(8,128)} %reshape.116.nodes, bf16[1024,96]{1,0:T(8,128)(2,1)} %constant.82.clone.inter, ...), custom_call_target="tpu_custom_call" | custom-call | tf_op jit(solution)/shard_map/tile/pallas_call | solution.py:314
  93.1 1.2 reshape.111
  94.3 0.4 copy.48
  94.7 0.3 fusion.4
  95.0 0.3 fusion.2
  95.3 0.2 multiply_add_fusion.8
  95.5 0.1 multiply_add_fusion.5
  95.6 0.1 multiply_add_fusion.2
  95.8 0.1 fusion.10
  96.0 0.3 fusion.11
  96.3 0.0 copy-start.3
  96.3 0.3 fusion.12
  96.6 0.4 bitcast_add_fusion
  97.0 0.4 copy.49
  97.4 0.0 copy-done.3
  97.4 0.3 reshape.113
  97.7 0.5 copy.50
  98.2 0.1 pad_maximum_fusion.1
  98.3 1.9 %collective-permute-start.2 = (f32[2,3,17,17]{3,0,2,1:T(2,128)S(1)}, f32[2,3,17,17]{3,0,2,1:T(2,128)S(1)}, u32[]{:S(2)}, u32[]{:S(2)}) collective-permute-start(f32[2,3,17,17]{3,0,2,1:T(2,128)S(1)} %bitcast.41), channel_id=1, source_target_pairs={{0,4},{4,8},{8,12},{12,16},{16,20},{20,24},{24,28},{1,5},{5,9},{9,... | collective-permute-start | bytes 20816 | tf_op jit(solution)/shard_map/ppermute | solution.py:25
  100.3 0.1 fusion
  100.3 4.3 %collective-permute-done.2 = f32[2,3,17,17]{3,0,2,1:T(2,128)S(1)} collective-permute-done((f32[2,3,17,17]{3,0,2,1:T(2,128)S(1)}, f32[2,3,17,17]{3,0,2,1:T(2,128)S(1)}, u32[]{:S(2)}, u32[]{:S(2)}) %collective-permute-start.2) | collective-permute-done | bytes 6968 | tf_op jit(solution)/shard_map/ppermute | solution.py:25
  104.7 0.1 fusion.7
  104.7 0.2 scatter-add.6
  105.0 0.3 slice.248
  105.3 0.0 copy-start.2
  105.3 0.7 copy.53
  106.0 3.5 %collective-permute-start.3 = (f32[2,3,17,16]{2,3,1,0:T(8,128)S(1)}, f32[2,3,17,16]{2,3,1,0:T(8,128)S(1)}, u32[]{:S(2)}, u32[]{:S(2)}) collective-permute-start(f32[2,3,17,16]{2,3,1,0:T(8,128)S(1)} %bitcast.43), channel_id=1, source_target_pairs={{0,1},{1,2},{2,3},{4,5},{5,6},{6,7},{8,9},{9,10},{10,11},{12,13},{... | collective-permute-start | bytes 19592 | tf_op jit(solution)/shard_map/ppermute | solution.py:25
  109.4 2.5 %collective-permute-done.3 = f32[2,3,17,16]{2,3,1,0:T(8,128)S(1)} collective-permute-done((f32[2,3,17,16]{2,3,1,0:T(8,128)S(1)}, f32[2,3,17,16]{2,3,1,0:T(8,128)S(1)}, u32[]{:S(2)}, u32[]{:S(2)}) %collective-permute-start.3) | collective-permute-done | bytes 6560 | tf_op jit(solution)/shard_map/ppermute | solution.py:25
  111.9 0.7 copy.54
  112.6 0.1 slice_add_fusion
  112.7 6.7 %scatter-add.9 = f32[2,3,17,16,16]{4,3,2,1,0:T(8,128)S(1)} dynamic-update-slice(f32[2,3,17,16,16]{4,3,2,1,0:T(8,128)S(1)} %bitcast.29, f32[2,3,17,16,1]{4,3,2,1,0:T(8,128)S(1)} %slice_add_fusion, s32[]{:T(128)} %constant.80.clone.1, s32[]{:T(128)} %constant.80.clone.1, s32[]{:T(128)} %constant.80.clone.1, s32[]{:T(128)} %constant.80.clone.1, s32[]{:T(128)} %constant.80.clone.1) | dynamic-update-slice | bytes 13060 | tf_op jit(solution)/shard_map/scatter-add | solution.py:382
  119.5 0.1 fusion.1
  119.5 0.4 copy.55
  119.9 0.0 copy-done.2
  119.9 0.8 bitcast_subtract_fusion
  (5 shorter events, 0.2 us)
Async XLA Ops:
  1.4 4.3 %collective-permute-start = (f32[3,17,16]{1,2,0:T(8,128)S(1)}, f32[3,17,16]{1,2,0:T(8,128)S(1)}, u32[]{:S(2)}, u32[]{:S(2)}) collective-permute-start(f32[3,17,16]{1,2,0:T(8,128)S(1)} %slice_bitcast_fusion), channel_id=1, source_target_pairs={{4,0},{8,4},{12,8},{16,12},{20,16},{24,20},{28,24},{5,1},{9,5},{13... | collective-permute-start | bytes 9800 | tf_op jit(solution)/shard_map/ppermute | solution.py:25
  6.1 53.9 %collective-permute-start.1 = (f32[3,17,17]{2,1,0:T(8,128)S(1)}, f32[3,17,17]{2,1,0:T(8,128)S(1)}, u32[]{:S(2)}, u32[]{:S(2)}) collective-permute-start(f32[3,17,17]{2,1,0:T(8,128)S(1)} %fusion.9), channel_id=1, source_target_pairs={{1,0},{2,1},{3,2},{5,4},{6,5},{7,6},{9,8},{10,9},{11,10},{13,12},{... | collective-permute-start | bytes 10412 | tf_op jit(solution)/shard_map/ppermute | solution.py:25
  8.5 2.2 %copy-start.1 = (bf16[128,128,128]{2,1,0:T(8,128)(2,1)S(1)}, bf16[128,128,128]{2,1,0:T(8,128)(2,1)}, u32[]{:S(2)}) copy-start(bf16[128,128,128]{2,1,0:T(8,128)(2,1)} %own.1) | copy-start | bytes 12582916
  55.9 4.2 %copy-start = (bf16[194,224,128]{2,1,0:T(8,128)(2,1)}, bf16[194,224,128]{2,1,0:T(8,128)(2,1)S(1)}, u32[]{:S(2)}) copy-start(bf16[194,224,128]{2,1,0:T(8,128)(2,1)S(1)} %halo.1.ext) | copy-start | bytes 33374212
  96.3 1.1 copy-start.3
  98.3 6.3 %collective-permute-start.2 = (f32[2,3,17,17]{3,0,2,1:T(2,128)S(1)}, f32[2,3,17,17]{3,0,2,1:T(2,128)S(1)}, u32[]{:S(2)}, u32[]{:S(2)}) collective-permute-start(f32[2,3,17,17]{3,0,2,1:T(2,128)S(1)} %bitcast.41), channel_id=1, source_target_pairs={{0,4},{4,8},{8,12},{12,16},{16,20},{20,24},{24,28},{1,5},{5,9},{9,... | collective-permute-start | bytes 20816 | tf_op jit(solution)/shard_map/ppermute | solution.py:25
  105.3 14.6 %copy-start.2 = (f32[3,17,16,16]{1,3,2,0:T(8,128)S(1)}, f32[3,17,16,16]{1,3,2,0:T(8,128)}, u32[]{:S(2)}) copy-start(f32[3,17,16,16]{1,3,2,0:T(8,128)} %param.17) | copy-start | bytes 156676
  106.0 6.0 %collective-permute-start.3 = (f32[2,3,17,16]{2,3,1,0:T(8,128)S(1)}, f32[2,3,17,16]{2,3,1,0:T(8,128)S(1)}, u32[]{:S(2)}, u32[]{:S(2)}) collective-permute-start(f32[2,3,17,16]{2,3,1,0:T(8,128)S(1)} %bitcast.43), channel_id=1, source_target_pairs={{0,1},{1,2},{2,3},{4,5},{5,6},{6,7},{8,9},{9,10},{10,11},{12,13},{... | collective-permute-start | bytes 19592 | tf_op jit(solution)/shard_map/ppermute | solution.py:25
where the time goes:
time: 121 us
  Pallas kernels  75.5 us (62%)
  local copies, waits for them, and re-layouts  22.5 us (19%)
  starting transfers between devices  10.5 us (9%)
  waiting for transfers between devices  6.95 us (6%)
  other arithmetic  4.33 us (4%)
    pallas_call x1, Pallas kernels, exchange(): pl.pallas_call(functools.partial(halo_kernel, nw, nn, rim), out_shape=jax...  45.2 us
    pallas_call x1, Pallas kernels, tile_terms(): pl.pallas_call(functools.partial(tile_kernel, rim), grid_spec=grid_spec,...  30.4 us
    ppermute x4, starting transfers between devices, shifted(): return lax.ppermute(array, axis, pairs)  10.5 us
    unnamed x10, local copies, waits for them, and re-layouts  8.33 us
    ppermute x4, waiting for transfers between devices, shifted(): return lax.ppermute(array, axis, pairs)  6.95 us
    scatter-add x1, local copies, waits for them, and re-layouts, per_device(): both = both[:, :, :, :, :-1].at[:, :, :, :, 0].add(got_narrow)  6.71 us
  transfers between devices with their start and end apart: 4, of which 3 were waited for; matrix products, arithmetic and copies ran while one was open for 1% of the time, Pallas kernels for 37%

commit v1 on v0

v1 whole, which is shorter than its diff:
```python
import functools

import jax
import jax.numpy as jnp
import numpy as np
from jax import lax
from jax.experimental import pallas as pl
from jax.experimental.pallas import tpu as pltpu
from jax.sharding import PartitionSpec as P

MU_SHEAR = 1.0
LAMBDA_BULK = 2.0
REG_WEIGHT = 256.0
STIFFNESS = 16.0
MESH = pl.DeviceIdType.MESH
F32 = jnp.float32
BF16 = jnp.bfloat16
SIDE = 48
QPAD = 24


def as_int(flag):
    return flag.astype(jnp.int32)


def halo_kernel(nw, nn, rim, own, extra_in, edge_x, edge_y, ext, extra, edges,
                zeros, send, recv, zsem, lsem):
    rows, cols, _ = own.shape
    side = rim - 1
    w = lax.axis_index("wide")
    n = lax.axis_index("narrow")
    lo_w, hi_w, lo_n, hi_n = w > 0, w < nw - 1, n > 0, n < nn - 1
    up_w, dn_w = (w + 1, n), (w - 1, n)
    up_n, dn_n = (w, n + 1), (w, n - 1)
    mid = slice(side, side + cols)
    ylo = slice(0, side)
    yhi = slice(side + cols, 2 * side + cols)
    total = rows + 2 * rim
    emid = slice(SIDE, SIDE + rows)
    edges[...] = jnp.zeros_like(edges)
    extra[...] = jnp.zeros_like(extra)
    barrier = pltpu.get_barrier_semaphore()
    for there, device in ((lo_w, dn_w), (hi_w, up_w), (lo_n, dn_n), (hi_n, up_n)):
        @pl.when(there)
        def _(device=device):
            pl.semaphore_signal(barrier, inc=1, device_id=device, device_id_type=MESH)
    zeros[...] = jnp.zeros_like(zeros)
    jobs = []

    def fill(cond, dst):
        src = zeros.at[tuple(slice(0, d) for d in dst.shape)]
        jobs.append((cond, pltpu.make_async_copy(src, dst, zsem.at[len(jobs)])))

    for cond, span in ((jnp.logical_not(lo_n), ylo), (jnp.logical_not(hi_n), yhi)):
        fill(cond, ext.at[:, span])
    for cond, band in ((jnp.logical_not(lo_w), slice(0, rim)), (jnp.logical_not(hi_w), slice(rim + rows, total))):
        fill(cond, ext.at[band, mid])
        fill(cond & lo_n, ext.at[band, ylo])
        fill(cond & hi_n, ext.at[band, yhi])
    for cond, job in jobs:
        @pl.when(cond)
        def _(job=job):
            job.start()
    pl.semaphore_wait(barrier, as_int(lo_w) + as_int(hi_w) + as_int(lo_n) + as_int(hi_n))

    def remote(k, src, dst, device):
        return pltpu.make_async_remote_copy(
            src_ref=src, dst_ref=dst, send_sem=send.at[k], recv_sem=recv.at[k],
            device_id=device, device_id_type=MESH)

    first = [
        (lo_w, hi_w, remote(0, edge_x, edges.at[0], dn_w)),
        (lo_n, hi_n, remote(1, edge_y, edges.at[1], dn_n)),
        (hi_n, lo_n, remote(2, extra_in.at[0], extra.at[0, emid], up_n)),
        (lo_n, hi_n, remote(3, extra_in.at[1], extra.at[1, emid], dn_n)),
    ]
    full = (slice(0, rim), slice(rows - rim, rows), slice(rim, rows - rim))
    for j, part in enumerate(full):
        there = slice(part.start + rim, part.stop + rim)
        first.append((hi_n, lo_n, remote(4 + 2 * j, own.at[part, cols - side:cols], ext.at[there, ylo], up_n)))
        first.append((lo_n, hi_n, remote(5 + 2 * j, own.at[part, 0:side], ext.at[there, yhi], dn_n)))
    first.append((hi_w, lo_w, remote(10, own.at[rows - rim:rows], ext.at[0:rim, mid], up_w)))
    first.append((lo_w, hi_w, remote(11, own.at[0:rim], ext.at[rows + rim:total, mid], dn_w)))
    for goes, _c, copy in first:
        @pl.when(goes)
        def _(copy=copy):
            copy.start()
    local = pltpu.make_async_copy(own, ext.at[rim:rim + rows, mid], lsem)
    local.start()
    low_rows, high_rows = slice(rim, 2 * rim), slice(rows, rows + rim)
    below, above = slice(0, rim), slice(rim + rows, total)
    elow, ehigh = slice(SIDE, 2 * SIDE), slice(rows, SIDE + rows)
    ebelow, eabove = slice(0, SIDE), slice(SIDE + rows, 2 * SIDE + rows)
    second = {
        0: [(hi_w & lo_n, hi_w & hi_n, remote(12, edges.at[0], edges.at[2], dn_n))],
        2: [(lo_n & lo_w, lo_n & hi_w, remote(13, extra.at[0, elow], extra.at[0, eabove], dn_w)),
            (lo_n & hi_w, lo_n & lo_w, remote(14, extra.at[0, ehigh], extra.at[0, ebelow], up_w))],
        3: [(hi_n & lo_w, hi_n & hi_w, remote(15, extra.at[1, elow], extra.at[1, eabove], dn_w)),
            (hi_n & hi_w, hi_n & lo_w, remote(16, extra.at[1, ehigh], extra.at[1, ebelow], up_w))],
        4: [(lo_n & lo_w, lo_n & hi_w, remote(17, ext.at[low_rows, ylo], ext.at[above, ylo], dn_w))],
        5: [(hi_n & lo_w, hi_n & hi_w, remote(18, ext.at[low_rows, yhi], ext.at[above, yhi], dn_w))],
        6: [(lo_n & hi_w, lo_n & lo_w, remote(19, ext.at[high_rows, ylo], ext.at[below, ylo], up_w))],
        7: [(hi_n & hi_w, hi_n & lo_w, remote(20, ext.at[high_rows, yhi], ext.at[below, yhi], up_w))],
    }
    later = []
    for k, (_g, comes, copy) in enumerate(first):
        @pl.when(comes)
        def _(copy=copy):
            copy.wait_recv()
        for entry in second.get(k, ()):
            later.append(entry)
            @pl.when(entry[0])
            def _(entry=entry):
                entry[2].start()
    for _g, comes, copy in later:
        @pl.when(comes)
        def _(copy=copy):
            copy.wait_recv()
    for goes, _c, copy in first + later:
        @pl.when(goes)
        def _(copy=copy):
            copy.wait_send()
    for cond, job in jobs:
        @pl.when(cond)
        def _(job=job):
            job.wait()
    local.wait()


def exchange(deformed, by_node, nw, nn):
    rows, cols, layers = deformed.shape
    rim = rows // 4 + 1
    shape = (rows + 2 * rim, cols + 2 * (rim - 1), layers)
    extra_in = jnp.stack([deformed[:, cols - rim], deformed[:, rim - 1]])
    anywhere = pl.BlockSpec(memory_space=pl.ANY)
    near = pl.BlockSpec(memory_space=pltpu.VMEM)
    lanes = by_node.shape[-1]
    return pl.pallas_call(
        functools.partial(halo_kernel, nw, nn, rim),
        out_shape=[jax.ShapeDtypeStruct(shape, BF16),
                   jax.ShapeDtypeStruct((2, rows + 2 * SIDE, layers), BF16),
                   jax.ShapeDtypeStruct((3,) + by_node.shape[1:], F32)],
        in_specs=[anywhere, near, near, near],
        out_specs=[anywhere, near, near],
        scratch_shapes=[
            pltpu.VMEM((shape[0], cols, layers), BF16),
            pltpu.SemaphoreType.DMA((21,)),
            pltpu.SemaphoreType.DMA((21,)),
            pltpu.SemaphoreType.DMA((8,)),
            pltpu.SemaphoreType.DMA,
        ],
        compiler_params=pltpu.CompilerParams(
            collective_id=0, has_side_effects=True, vmem_limit_bytes=62 << 20),
        name="halo",
    )(deformed, extra_in, by_node[0], by_node[:, 0])


def tables(rows, cols, layers, comps):
    def one(voxels):
        t = np.zeros((voxels, voxels // 8 + 1))
        for i in range(voxels):
            f = (i % 8 + 0.5) / 8.0
            t[i, i // 8] += 1.0 - f
            t[i, i // 8 + 1] += f
        return t
    ty, tz = one(cols), one(layers)
    nq, ns = ty.shape[1], tz.shape[1]
    typ = np.zeros((cols, QPAD))
    typ[:, :nq] = ty
    frac = (np.arange(8) + 0.5) / 8.0
    wx = np.stack([1.0 - frac, frac], 1)
    inter = 0.5 * np.einsum("ka,yq->kyaq", wx, typ)
    inter = np.concatenate([inter[:, :, 0], inter[:, :, 0], inter[:, :, 1], inter[:, :, 1]], -1)
    inter = inter.reshape(8 * cols, 4 * QPAD)
    proj = np.concatenate([typ.T, typ.T], 1)
    diag = np.einsum("ka,yq->aqky", wx * wx, typ * typ).reshape(2 * QPAD, 8 * cols)
    dhi = diag.astype(BF16).astype(np.float64)
    diag = np.concatenate([dhi, diag - dhi], 0)
    lanes = comps * layers
    up = np.zeros((2 * 128, lanes))
    down = np.zeros((lanes, 128))
    down2 = np.zeros((lanes, 128))
    for c in range(comps):
        for h in range(2):
            up[h * 128 + c * ns:h * 128 + (c + 1) * ns, c * layers:(c + 1) * layers] = tz.T
        down[c * layers:(c + 1) * layers, c * ns:(c + 1) * ns] = -0.5 * tz
        down2[c * layers:(c + 1) * layers, c * ns:(c + 1) * ns] = 0.25 * tz * tz
    dz = np.zeros((layers, layers))
    for z in range(layers):
        if z + 1 < layers:
            dz[z + 1, z] = 1.0
        if z > 0:
            dz[z - 1, z] = -1.0
    as_bf16 = lambda a: jnp.asarray(a.astype(BF16))
    return [as_bf16(a) for a in (inter, proj, diag, up, down, down2, dz)]


def split(value):
    high = value.astype(BF16)
    return high, (value - high.astype(F32)).astype(BF16)


def strain_pull(ns, nodes, pull):
    npx = nodes.shape[0]
    nel = npx - 1
    lane = lax.broadcasted_iota(jnp.int32, (nel, 128), 1)
    move = lambda a, by: pltpu.roll(a, by % 128, 1)
    pull[...] = jnp.zeros_like(pull)

    @pl.loop(0, nel)
    def _(p):
        a00, a01 = nodes[p, 0:nel], nodes[p, 1:nel + 1]
        a10, a11 = nodes[p + 1, 0:nel], nodes[p + 1, 1:nel + 1]
        dx = (a10 - a00) + (a11 - a01)
        dy = (a01 - a00) + (a11 - a10)
        every = (a00 + a01) + (a10 + a11)
        slopes = (dx + move(dx, -1), dy + move(dy, -1), move(every, -1) - every)
        f = [[0.03125 * (move(h, -ns * i) if i else h) + (1.0 if i == j else 0.0)
              for j, h in enumerate(slopes)] for i in range(3)]
        cof = [[f[(i + 1) % 3][(j + 1) % 3] * f[(i + 2) % 3][(j + 2) % 3]
                - f[(i + 1) % 3][(j + 2) % 3] * f[(i + 2) % 3][(j + 1) % 3]
                for j in range(3)] for i in range(3)]
        ratio = f[0][0] * cof[0][0] + f[0][1] * cof[0][1] + f[0][2] * cof[0][2]
        factor = (LAMBDA_BULK * jnp.log(ratio) - MU_SHEAR) / ratio
        back = []
        for j in range(3):
            parts = [jnp.where(lane < ns - 1, MU_SHEAR * f[i][j] + factor * cof[i][j], 0.0) for i in range(3)]
            back.append((parts[0] + move(parts[1], ns) + move(parts[2], 2 * ns)) * (0.03125 * REG_WEIGHT))
        gx = back[0] + move(back[0], 1)
        gy = back[1] + move(back[1], 1)
        gz = move(back[2], 1) - back[2]
        for dp, dq in ((0, 0), (0, 1), (1, 0), (1, 1)):
            add = (gx if dp else -gx) + (gy if dq else -gy) + gz
            pull[p + dp, dq:dq + nel] = pull[p + dp, dq:dq + nel] + add


def tile_kernel(rim, ns, map_ref, ref_tile, ext, extra, by_node, edges,
                inter, proj, diag, up, down, down2, dz,
                res, out,
                rows_in, shift, samp, ndz, moved, gy, gz, sums, sq, gacc, dacc, nodes, pull, rimcol, sem):
    p = pl.program_id(0)
    steps = pl.num_programs(0)
    cols, layers = samp.shape[1], samp.shape[2]
    comps = ndz.shape[2] // layers
    side = rim - 1
    wide_cols = cols + 2 * side
    start = map_ref[0] + side

    def fetch(first, count, k):
        return pltpu.make_async_copy(
            ext.at[pl.ds(start + first, count)],
            rows_in.at[pl.ds(first, count), 0:wide_cols], sem.at[k])

    def sample(first, count):
        for a in range(count):
            at = map_ref[0] + (SIDE - 1) + first + a
            which = lax.broadcasted_iota(jnp.int32, (16, layers), 0)
            low = jnp.broadcast_to(rimcol[0, pl.ds(at, 1), :], (16, layers))
            high = jnp.broadcast_to(rimcol[1, pl.ds(at, 1), :], (16, layers))
            rows_in[first + a, wide_cols:wide_cols + 16] = jnp.where(
                which == 0, low, jnp.where(which == 1, high, 0.0)).astype(BF16)
        for a in range(0, count, 2):
            pair = jnp.concatenate([rows_in[first + a], rows_in[first + a + 1]], axis=1)
            got = jnp.dot(shift[...], pair, preferred_element_type=F32)
            for b in range(2):
                samp[first + a + b] = got[:cols, b * layers:(b + 1) * layers]
                gy[(first + a + b) % 16] = got[cols:, b * layers:(b + 1) * layers]

    @pl.when(p == 0)
    def _():
        fetch(0, 2, steps).start()

        @pl.loop(0, steps)
        def _(k):
            fetch(8 * k + 2, 8, k).start()
        rimcol[...] = extra[...].astype(F32)
        y = lax.broadcasted_iota(jnp.int32, (cols, shift.shape[1]), 0)
        k = lax.broadcasted_iota(jnp.int32, (cols, shift.shape[1]), 1)
        place = jnp.where(k < wide_cols, k - side,
                          jnp.where(k == wide_cols, -side - 1,
                                    jnp.where(k == wide_cols + 1, cols + side, 1 << 20)))
        gap = place - y - map_ref[1]
        shift[:cols] = jnp.where(gap == 0, 1.0, 0.0).astype(BF16)
        shift[cols:] = (jnp.where(gap == 1, 1.0, 0.0) - jnp.where(gap == -1, 1.0, 0.0)).astype(BF16)
        nel = by_node.shape[0]
        nodes[0:nel, 0:nel] = by_node[...]
        nodes[nel, 0:nel] = edges[0]
        top = lax.broadcasted_iota(jnp.int32, (QPAD - nel, 128), 0) == 0
        for i in range(nel + 1):
            row = edges[1, i:i + 1] if i < nel else edges[2, 0:1]
            nodes[i, nel:QPAD] = jnp.where(top, jnp.broadcast_to(row, (QPAD - nel, 128)), 0.0)
        flat = nodes[...].reshape(-1, 128)
        high = flat.astype(BF16).astype(F32)
        both = jnp.concatenate([high, flat - high], axis=1).astype(BF16)
        level = jnp.dot(both, up[...], preferred_element_type=F32)
        for i in range(ndz.shape[0]):
            part = level[i * QPAD:(i + 1) * QPAD]
            head = part.astype(BF16).astype(F32)
            ndz[i] = jnp.concatenate([head, part - head], axis=0).astype(BF16)
        strain_pull(ns, nodes, pull)
        gacc[...] = jnp.zeros_like(gacc)
        dacc[...] = jnp.zeros_like(dacc)
        fetch(0, 2, steps).wait()
        sample(0, 2)

    base = pl.multiple_of(8 * p, 8)
    fetch(base + 2, 8, p).wait()
    sample(base + 2, 8)
    gz[...] = jnp.dot(samp[pl.ds(base + 1, 8)].reshape(8 * cols, layers).astype(BF16), dz[...],
                      preferred_element_type=F32)
    level = ndz[pl.ds(p, 2)].reshape(4 * QPAD, comps * layers)
    moved[...] = jnp.dot(inter[...], level, preferred_element_type=F32)

    chunk = 32

    @pl.loop(0, cols // chunk)
    def _(j):
        at = pl.multiple_of(j * chunk, chunk)
        span = pl.ds(at, chunk)
        run = [None] * comps
        tot = [None] * comps
        for k in range(8):
            line = pl.ds(k * cols + at, chunk)
            here = samp[base + 1 + k, span, :]
            g = [samp[base + 2 + k, span, :] - samp[base + k, span, :],
                 gy[(base + 1 + k) % 16, span, :],
                 gz[line, :]]
            r = ref_tile[k, span, :].astype(F32) - here
            for c in range(3):
                r = r - g[c] * moved[line, c * layers:(c + 1) * layers]
            res[k, span, :] = r.astype(BF16)
            for c in range(3):
                f = g[c] * r
                run[c] = f if k == 0 else run[c] + f
                tot[c] = run[c] if k == 0 else tot[c] + run[c]
                sq[line, c * layers:(c + 1) * layers] = (g[c] * g[c]).astype(BF16)
        for c in range(3):
            low = (tot[c] - 0.5 * run[c]) * 0.125
            for a, value in enumerate((low, run[c] - low)):
                head, tail = split(value)
                sums[a, span, c * layers:(c + 1) * layers] = head
                sums[a, pl.ds(cols + at, chunk), c * layers:(c + 1) * layers] = tail

    for a in range(2):
        gacc[p + a] = gacc[p + a] + jnp.dot(proj[...], sums[a], preferred_element_type=F32)
    got = jnp.dot(diag[...], sq[...], preferred_element_type=F32)
    for a in range(2):
        dacc[p + a] = dacc[p + a] + (got[a * QPAD:(a + 1) * QPAD] + got[(2 + a) * QPAD:(3 + a) * QPAD])

    @pl.when(p == steps - 1)
    def _():
        for k, (acc, table) in enumerate(((gacc, down), (dacc, down2))):
            head, tail = split(acc[...].reshape(-1, comps * layers))
            got = (jnp.dot(head, table[...], preferred_element_type=F32)
                   + jnp.dot(tail, table[...], preferred_element_type=F32)).reshape(pull.shape)
            out[k] = got + pull[...] if k == 0 else got


def tile_terms(reference_tile, ext, extra, by_node, edges, offsets, ns):
    rows, cols, layers = reference_tile.shape
    comps = 3
    npx = by_node.shape[0] + 1
    rim = rows // 4 + 1
    tabs = tables(rows, cols, layers, comps)
    steps = rows // 8
    whole = lambda a: pl.BlockSpec(a.shape, lambda p, m: (0,) * a.ndim, pipeline_mode=pl.Buffered(1))
    slab = pl.BlockSpec((8, cols, layers), lambda p, m: (p, 0, 0))
    out_nodes = jax.ShapeDtypeStruct((2, npx, QPAD, 128), F32)
    depth = cols + 2 * (rim - 1) + 16
    grid_spec = pltpu.PrefetchScalarGridSpec(
        num_scalar_prefetch=1,
        grid=(steps,),
        in_specs=[slab, pl.BlockSpec(memory_space=pl.ANY), whole(extra), whole(by_node), whole(edges)]
        + [whole(t) for t in tabs],
        out_specs=[slab, whole(out_nodes)],
        scratch_shapes=[
            pltpu.VMEM((rows + 2, depth, layers), BF16),
            pltpu.VMEM((2 * cols, depth), BF16),
            pltpu.VMEM((rows + 2, cols, layers), F32),
            pltpu.VMEM((npx, 2 * QPAD, comps * layers), BF16),
            pltpu.VMEM((8 * cols, comps * layers), F32),
            pltpu.VMEM((16, cols, layers), F32),
            pltpu.VMEM((8 * cols, layers), F32),
            pltpu.VMEM((2, 2 * cols, comps * layers), BF16),
            pltpu.VMEM((8 * cols, comps * layers), BF16),
            pltpu.VMEM((npx, QPAD, comps * layers), F32),
            pltpu.VMEM((npx, QPAD, comps * layers), F32),
            pltpu.VMEM((npx, QPAD, 128), F32),
            pltpu.VMEM((npx, QPAD, 128), F32),
            pltpu.VMEM(extra.shape, F32),
            pltpu.SemaphoreType.DMA((steps + 1,)),
        ],
    )
    return pl.pallas_call(
        functools.partial(tile_kernel, rim, ns),
        grid_spec=grid_spec,
        out_shape=[jax.ShapeDtypeStruct(reference_tile.shape, BF16), out_nodes],
        compiler_params=pltpu.CompilerParams(
            dimension_semantics=("arbitrary",), vmem_limit_bytes=62 << 20),
        name="tile",
    )(offsets, reference_tile, ext, extra, by_node, edges, *tabs)


def node_kernel(nw, nn, terms, by_node, out, column, from_w, from_n, from_c, send, recv):
    nel = by_node.shape[0]
    w = lax.axis_index("wide")
    n = lax.axis_index("narrow")
    lo_w, hi_w, lo_n, hi_n = w > 0, w < nw - 1, n > 0, n < nn - 1
    up_w, dn_w = (w + 1, n), (w - 1, n)
    up_n, dn_n = (w, n + 1), (w, n - 1)
    for ref in (from_w, from_n, from_c):
        ref[...] = jnp.zeros_like(ref)
    barrier = pltpu.get_barrier_semaphore()
    for there, device in ((lo_w, dn_w), (hi_w, up_w), (lo_n, dn_n), (hi_n, up_n)):
        @pl.when(there)
        def _(device=device):
            pl.semaphore_signal(barrier, inc=1, device_id=device, device_id_type=MESH)
    for k in range(2):
        for p in range(nel):
            column[k, p:p + 1] = terms[k, p, nel:nel + 1]
    pl.semaphore_wait(barrier, as_int(lo_w) + as_int(hi_w) + as_int(lo_n) + as_int(hi_n))

    def remote(k, src, dst, device):
        return pltpu.make_async_remote_copy(
            src_ref=src, dst_ref=dst, send_sem=send.at[k], recv_sem=recv.at[k],
            device_id=device, device_id_type=MESH)

    wide_copy = remote(0, terms.at[:, nel], from_w, up_w)
    narrow_copy = remote(1, column, from_n, up_n)
    corner_copy = remote(2, from_w.at[:, nel:QPAD], from_c, up_n)

    @pl.when(hi_w)
    def _():
        wide_copy.start()

    @pl.when(hi_n)
    def _():
        narrow_copy.start()

    @pl.when(lo_w)
    def _():
        wide_copy.wait_recv()

    @pl.when(lo_w & hi_n)
    def _():
        corner_copy.start()

    @pl.when(lo_n)
    def _():
        narrow_copy.wait_recv()

    @pl.when(lo_w & lo_n)
    def _():
        corner_copy.wait_recv()

    top = lax.broadcasted_iota(jnp.int32, (nel, 128), 0) == 0
    for p in range(nel):
        sums = []
        for k in range(2):
            value = terms[k, p, 0:nel]
            side = from_n[k, p:p + 1]
            if p == 0:
                value = value + from_w[k, 0:nel]
                side = side + from_c[k, 0:1]
            sums.append(value + jnp.where(top, jnp.broadcast_to(side, (nel, 128)), 0.0))
        out[p] = by_node[p] - sums[0] / (sums[1] + STIFFNESS)

    @pl.when(hi_w)
    def _():
        wide_copy.wait_send()

    @pl.when(hi_n)
    def _():
        narrow_copy.wait_send()

    @pl.when(lo_w & hi_n)
    def _():
        corner_copy.wait_send()


def node_update(terms, by_node, nw, nn):
    nel = by_node.shape[0]
    near = pl.BlockSpec(memory_space=pltpu.VMEM)
    return pl.pallas_call(
        functools.partial(node_kernel, nw, nn),
        out_shape=jax.ShapeDtypeStruct(by_node.shape, F32),
        in_specs=[near, near],
        out_specs=near,
        scratch_shapes=[
            pltpu.VMEM((2, nel, 128), F32),
            pltpu.VMEM((2, QPAD, 128), F32),
            pltpu.VMEM((2, nel, 128), F32),
            pltpu.VMEM((2, QPAD - nel, 128), F32),
            pltpu.SemaphoreType.DMA((3,)),
            pltpu.SemaphoreType.DMA((3,)),
        ],
        compiler_params=pltpu.CompilerParams(collective_id=1, has_side_effects=True),
        name="nodes",
    )(terms, by_node)


def per_device(nw, nn, reference_image, deformed_image, displacement, tile_map):
    comps, ns, nex, ney = displacement.shape
    by_node = displacement.transpose(2, 3, 0, 1).reshape(nex, ney, comps * ns)
    by_node = jnp.pad(by_node, ((0, 0), (0, 0), (0, 128 - comps * ns)))
    ext, extra, edges = exchange(deformed_image, by_node, nw, nn)
    residual, terms = tile_terms(
        reference_image, ext, extra, by_node, edges, tile_map.reshape(2), ns)
    moved = node_update(terms, by_node, nw, nn)
    updated = moved[:, :, :comps * ns].reshape(nex, ney, comps, ns).transpose(2, 3, 0, 1)
    return (updated, residual)


def solution(mesh):
    placed = (
        P("wide", "narrow", None),
        P("wide", "narrow", None),
        P(None, None, "wide", "narrow"),
        P("wide", "narrow", None),
    )
    return jax.shard_map(
        functools.partial(per_device, mesh.shape["wide"], mesh.shape["narrow"]),
        mesh=mesh,
        in_specs=placed,
        out_specs=(P(None, None, "wide", "narrow"), P("wide", "narrow", None)),
        check_vma=False,
    )
```

time: 121 us -> 183 us (1.51)
  Pallas kernels: 75.5 us -> 175 us
  local copies, waits for them, and re-layouts: 22.5 us -> 6.42 us
  starting transfers between devices: 10.5 us -> 0 us
  waiting for transfers between devices: 6.95 us -> 0 us
  other arithmetic: 4.33 us -> 0.64 us
    pallas_call x2 -> x3, Pallas kernels: 75.5 us -> 175 us  [the longest x1 132 us: exchange(): pl.pallas_call(functools.partial(halo_kernel, nw, nn, rim), out_shape=[ja...]
    ppermute x4 -> x0, starting transfers between devices: 10.5 us -> none  [shifted(): return lax.ppermute(array, axis, pairs)]
    unnamed x10 -> x1, local copies, waits for them, and re-layouts: 8.33 us -> 0.78 us
    ppermute x4 -> x0, waiting for transfers between devices: 6.95 us -> none  [shifted(): return lax.ppermute(array, axis, pairs)]
    scatter-add x2 -> x0, local copies, waits for them, and re-layouts: 6.95 us -> none  [the longest x1 6.71 us: per_device(): both = both[:, :, :, :, :-1].at[:, :, :, :, 0].add(got_narrow)]
  transfers between devices with their start and end apart: 4 -> 0, of which waited for: 3 -> 0; matrix products, arithmetic and copies ran while one was open for 1% -> 0% of each run, Pallas kernels for 37% -> 0%
where the time goes in v1:
time: 183 us
  Pallas kernels  175 us (96%)
  local copies, waits for them, and re-layouts  6.42 us (4%)
    pallas_call x1, Pallas kernels, exchange(): pl.pallas_call(functools.partial(halo_kernel, nw, nn, rim), out_shape=[ja...  132 us
    pallas_call x1, Pallas kernels, tile_terms(): pl.pallas_call(functools.partial(tile_kernel, rim, ns), grid_spec=grid_sp...  35.6 us
    pallas_call x1, Pallas kernels, node_update(): pl.pallas_call(functools.partial(node_kernel, nw, nn), out_shape=jax.Shap...  7.99 us

profile of v1, /device:TPU:12, one launch (start us, length us, event | category | flops | bytes accessed | tf_op | source)
XLA Modules:
  0.0 183.0 jit_solution(1344105966089437252)
XLA Ops:
  0.6 1.1 fusion
  1.8 0.6 pad_maximum_fusion.extra_in
  2.4 1.3 copy.19
  3.7 0.2 reshape.14
  3.9 0.6 slice_bitcast_fusion.edge_x
  4.5 0.6 pad_slice_fusion
  5.1 0.7 pad.4.by_node
  5.8 131.7 %halo.1 = (bf16[194,192,128]{2,1,0:T(8,128)(2,1)}, bf16[2,224,128]{2,1,0:T(8,128)(2,1)}, f32[3,16,128]{2,1,0:T(8,128)}) custom-call(bf16[128,128,128]{2,1,0:T(8,128)(2,1)} %own.1, bf16[2,128,128]{2,1,0:T(8,128)(2,1)} %pad_maximum_fusion.extra_in, f32[16,128]{1,0:T(8,128)} %slice_bitcast_fusion.edge_x, f32[16,128]{1,0:T(8,128)} %bitcast.14), custom_call_target="tpu_custom_call" | custom-call | tf_op jit(solution)/shard_map/halo/pallas_call | solution.py:138
  137.5 35.6 %tile.1 = (bf16[128,128,128]{2,1,0:T(8,128)(2,1)}, f32[2,17,24,128]{3,2,1,0:T(8,128)}) custom-call(s32[2]{0:T(128)} %bitcast.15, bf16[128,128,128]{2,1,0:T(8,128)(2,1)} %ref_tile.1, bf16[194,192,128]{2,1,0:T(8,128)(2,1)} %get-tuple-element.7.ext, bf16[2,224,128]{2,1,0:T(8,128)(2,1)} %get-tuple-element.8.extra, f32[16,16,128]{2,1,0:T(8,128)} %pad.4.by_node, ...), custom_call_target="tpu_custom_call" | custom-call | tf_op jit(solution)/shard_map/tile/pallas_call | solution.py:394
  173.1 8.0 %nodes.1 = f32[16,16,128]{2,1,0:T(8,128)} custom-call(f32[2,17,24,128]{3,2,1,0:T(8,128)} %get-tuple-element.10.terms, f32[16,16,128]{2,1,0:T(8,128)} %pad.4.by_node), custom_call_target="tpu_custom_call" | custom-call | tf_op jit(solution)/shard_map/nodes/pallas_call | solution.py:484
  181.1 1.1 reshape.15
  182.2 0.8 copy.20
  (1 shorter events, 0.0 us)

commit v2 on v1

--- a/solution.py
+++ b/solution.py
@@ -23,8 +23,8 @@
     return flag.astype(jnp.int32)
 
 
-def halo_kernel(nw, nn, rim, own, extra_in, edge_x, edge_y, ext, extra, edges,
-                zeros, send, recv, zsem, lsem):
+def halo_kernel(nw, nn, rim, own, extra_in, edge_x, edge_y, out, extra, edges,
+                ext, zeros, send, recv, zsem, lsem):
     rows, cols, _ = own.shape
     side = rim - 1
     w = lax.axis_index("wide")
@@ -37,6 +37,8 @@
     yhi = slice(side + cols, 2 * side + cols)
     total = rows + 2 * rim
     emid = slice(SIDE, SIDE + rows)
+    local = pltpu.make_async_copy(own, ext.at[rim:rim + rows, mid], lsem.at[0])
+    local.start()
     edges[...] = jnp.zeros_like(edges)
     extra[...] = jnp.zeros_like(extra)
     barrier = pltpu.get_barrier_semaphore()
@@ -77,16 +79,23 @@
     full = (slice(0, rim), slice(rows - rim, rows), slice(rim, rows - rim))
     for j, part in enumerate(full):
         there = slice(part.start + rim, part.stop + rim)
-        first.append((hi_n, lo_n, remote(4 + 2 * j, own.at[part, cols - side:cols], ext.at[there, ylo], up_n)))
-        first.append((lo_n, hi_n, remote(5 + 2 * j, own.at[part, 0:side], ext.at[there, yhi], dn_n)))
-    first.append((hi_w, lo_w, remote(10, own.at[rows - rim:rows], ext.at[0:rim, mid], up_w)))
-    first.append((lo_w, hi_w, remote(11, own.at[0:rim], ext.at[rows + rim:total, mid], dn_w)))
+        first.append((hi_n, lo_n, remote(4 + 2 * j, ext.at[there, cols:cols + side], ext.at[there, ylo], up_n)))
+        first.append((lo_n, hi_n, remote(5 + 2 * j, ext.at[there, side:2 * side], ext.at[there, yhi], dn_n)))
+    first.append((hi_w, lo_w, remote(10, ext.at[rows:rows + rim, mid], ext.at[0:rim, mid], up_w)))
+    first.append((lo_w, hi_w, remote(11, ext.at[rim:2 * rim, mid], ext.at[rows + rim:total, mid], dn_w)))
+    local.wait()
+    saves = []
+
+    def settle(k, span, columns):
+        save = pltpu.make_async_copy(ext.at[span, columns], out.at[span, columns], lsem.at[1 + k])
+        save.start()
+        saves.append(save)
+
     for goes, _c, copy in first:
         @pl.when(goes)
         def _(copy=copy):
             copy.start()
-    local = pltpu.make_async_copy(own, ext.at[rim:rim + rows, mid], lsem)
-    local.start()
+    settle(0, slice(rim, rim + rows), mid)
     low_rows, high_rows = slice(rim, 2 * rim), slice(rows, rows + rim)
     below, above = slice(0, rim), slice(rim + rows, total)
     elow, ehigh = slice(SIDE, 2 * SIDE), slice(rows, SIDE + rows)
@@ -116,15 +125,20 @@
         @pl.when(comes)
         def _(copy=copy):
             copy.wait_recv()
+    for cond, job in jobs:
+        @pl.when(cond)
+        def _(job=job):
+            job.wait()
+    settle(1, below, mid)
+    settle(2, above, mid)
+    settle(3, slice(0, total), ylo)
+    settle(4, slice(0, total), yhi)
     for goes, _c, copy in first + later:
         @pl.when(goes)
         def _(copy=copy):
             copy.wait_send()
-    for cond, job in jobs:
-        @pl.when(cond)
-        def _(job=job):
-            job.wait()
-    local.wait()
+    for save in saves:
+        save.wait()
 
 
 def exchange(deformed, by_node, nw, nn):
@@ -143,11 +157,12 @@
         in_specs=[anywhere, near, near, near],
         out_specs=[anywhere, near, near],
         scratch_shapes=[
+            pltpu.VMEM(shape, BF16),
             pltpu.VMEM((shape[0], cols, layers), BF16),
             pltpu.SemaphoreType.DMA((21,)),
             pltpu.SemaphoreType.DMA((21,)),
             pltpu.SemaphoreType.DMA((8,)),
-            pltpu.SemaphoreType.DMA,
+            pltpu.SemaphoreType.DMA((6,)),
         ],
         compiler_params=pltpu.CompilerParams(
             collective_id=0, has_side_effects=True, vmem_limit_bytes=62 << 20),

time: 183 us -> 95.3 us (0.52)
  Pallas kernels: 175 us -> 87.2 us
    pallas_call x1, Pallas kernels: 132 us -> 43.2 us  [exchange(): pl.pallas_call(functools.partial(halo_kernel, nw, nn, rim), out_shape=[ja...]
where the time goes in v2:
time: 95.3 us; the launch traced here: 95 us
  Pallas kernels  87.2 us (92%)
  local copies, waits for them, and re-layouts  6.42 us (7%)
    pallas_call x1, Pallas kernels, exchange(): pl.pallas_call(functools.partial(halo_kernel, nw, nn, rim), out_shape=[ja...  43.2 us
    pallas_call x1, Pallas kernels, tile_terms(): pl.pallas_call(functools.partial(tile_kernel, rim, ns), grid_spec=grid_sp...  35.5 us
    pallas_call x1, Pallas kernels, node_update(): pl.pallas_call(functools.partial(node_kernel, nw, nn), out_shape=jax.Shap...  8.51 us

profile of v2, /device:TPU:12, one launch (start us, length us, event | category | flops | bytes accessed | tf_op | source)
XLA Modules:
  0.0 95.0 jit_solution(10676419493933019458)
XLA Ops:
  0.6 1.1 %fusion = (bf16[128,1,128]{2,1,0:T(2,128)(2,1)S(1)}, bf16[128,1,128]{2,1,0:T(2,128)(2,1)S(1)}) fusion(bf16[128,128,128]{2,1,0:T(8,128)(2,1)} %own.1), kind=kLoop, calls=%fused_computation.5 | loop fusion | bytes 131072 | tf_op jit(solution)/shard_map/slice | solution.py:148
  1.8 0.6 pad_maximum_fusion.extra_in
  2.4 1.3 %copy.19 = f32[16,16,3,17]{3,2,1,0:T(4,128)S(1)} copy(f32[16,16,3,17]{3,1,0,2:T(8,128)} %bitcast.13) | data formatting | bytes 104448 | tf_op jit(solution)/shard_map/transpose | solution.py:519
  3.7 0.2 reshape.14
  3.9 0.6 slice_bitcast_fusion.edge_x
  4.5 0.6 pad_slice_fusion
  5.1 0.7 pad.4.by_node
  5.8 43.2 %halo.1 = (bf16[194,192,128]{2,1,0:T(8,128)(2,1)}, bf16[2,224,128]{2,1,0:T(8,128)(2,1)}, f32[3,16,128]{2,1,0:T(8,128)}) custom-call(bf16[128,128,128]{2,1,0:T(8,128)(2,1)} %own.1, bf16[2,128,128]{2,1,0:T(8,128)(2,1)} %pad_maximum_fusion.extra_in, f32[16,128]{1,0:T(8,128)} %slice_bitcast_fusion.edge_x, f32[16,128]{1,0:T(8,128)} %bitcast.14), custom_call_target="tpu_custom_call" | custom-call | tf_op jit(solution)/shard_map/halo/pallas_call | solution.py:152
  49.0 35.5 %tile.1 = (bf16[128,128,128]{2,1,0:T(8,128)(2,1)}, f32[2,17,24,128]{3,2,1,0:T(8,128)}) custom-call(s32[2]{0:T(128)} %bitcast.15, bf16[128,128,128]{2,1,0:T(8,128)(2,1)} %ref_tile.1, bf16[194,192,128]{2,1,0:T(8,128)(2,1)} %get-tuple-element.7.ext, bf16[2,224,128]{2,1,0:T(8,128)(2,1)} %get-tuple-element.8.extra, f32[16,16,128]{2,1,0:T(8,128)} %pad.4.by_node, ...), custom_call_target="tpu_custom_call" | custom-call | tf_op jit(solution)/shard_map/tile/pallas_call | solution.py:409
  84.5 8.5 %nodes.1 = f32[16,16,128]{2,1,0:T(8,128)} custom-call(f32[2,17,24,128]{3,2,1,0:T(8,128)} %get-tuple-element.10.terms, f32[16,16,128]{2,1,0:T(8,128)} %pad.4.by_node), custom_call_target="tpu_custom_call" | custom-call | tf_op jit(solution)/shard_map/nodes/pallas_call | solution.py:499
  93.0 1.1 %reshape.15 = f32[16,16,3,17]{3,2,1,0:T(4,128)S(1)} reshape(f32[16,16,51]{2,1,0:T(8,128)} %bitcast.12) | data formatting | bytes 104448 | tf_op jit(solution)/shard_map/reshape | solution.py:525
  94.2 0.8 copy.20
  (1 shorter events, 0.0 us)

commit v3 on v2

--- a/solution.py
+++ b/solution.py
@@ -23,8 +23,52 @@
     return flag.astype(jnp.int32)
 
 
-def halo_kernel(nw, nn, rim, own, extra_in, edge_x, edge_y, out, extra, edges,
-                ext, zeros, send, recv, zsem, lsem):
+def fill_nodes(nodes, by_node, edges):
+    nel = by_node.shape[0]
+    nodes[0:nel, 0:nel] = by_node[...]
+    nodes[nel, 0:nel] = edges[0]
+    top = lax.broadcasted_iota(jnp.int32, (QPAD - nel, 128), 0) == 0
+    for i in range(nel + 1):
+        row = edges[1, i:i + 1] if i < nel else edges[2, 0:1]
+        nodes[i, nel:QPAD] = jnp.where(top, jnp.broadcast_to(row, (QPAD - nel, 128)), 0.0)
+
+
+def strain_pull(ns, nodes, pull):
+    npx = nodes.shape[0]
+    nel = npx - 1
+    lane = lax.broadcasted_iota(jnp.int32, (nel, 128), 1)
+    move = lambda a, by: pltpu.roll(a, by % 128, 1)
+    pull[...] = jnp.zeros_like(pull)
+
+    @pl.loop(0, nel)
+    def _(p):
+        a00, a01 = nodes[p, 0:nel], nodes[p, 1:nel + 1]
+        a10, a11 = nodes[p + 1, 0:nel], nodes[p + 1, 1:nel + 1]
+        dx = (a10 - a00) + (a11 - a01)
+        dy = (a01 - a00) + (a11 - a10)
+        every = (a00 + a01) + (a10 + a11)
+        slopes = (dx + move(dx, -1), dy + move(dy, -1), move(every, -1) - every)
+        f = [[0.03125 * (move(h, -ns * i) if i else h) + (1.0 if i == j else 0.0)
+              for j, h in enumerate(slopes)] for i in range(3)]
+        cof = [[f[(i + 1) % 3][(j + 1) % 3] * f[(i + 2) % 3][(j + 2) % 3]
+                - f[(i + 1) % 3][(j + 2) % 3] * f[(i + 2) % 3][(j + 1) % 3]
+                for j in range(3)] for i in range(3)]
+        ratio = f[0][0] * cof[0][0] + f[0][1] * cof[0][1] + f[0][2] * cof[0][2]
+        factor = (LAMBDA_BULK * jnp.log(ratio) - MU_SHEAR) / ratio
+        back = []
+        for j in range(3):
+            parts = [jnp.where(lane < ns - 1, MU_SHEAR * f[i][j] + factor * cof[i][j], 0.0) for i in range(3)]
+            back.append((parts[0] + move(parts[1], ns) + move(parts[2], 2 * ns)) * (0.03125 * REG_WEIGHT))
+        gx = back[0] + move(back[0], 1)
+        gy = back[1] + move(back[1], 1)
+        gz = move(back[2], 1) - back[2]
+        for dp, dq in ((0, 0), (0, 1), (1, 0), (1, 1)):
+            add = (gx if dp else -gx) + (gy if dq else -gy) + gz
+            pull[p + dp, dq:dq + nel] = pull[p + dp, dq:dq + nel] + add
+
+
+def halo_kernel(nw, nn, rim, ns, own, extra_in, edge_x, edge_y, by_node, out, extra, nodes, pull,
+                edges, ext, zeros, send, recv, zsem, lsem):
     rows, cols, _ = own.shape
     side = rim - 1
     w = lax.axis_index("wide")
@@ -78,11 +122,12 @@
     ]
     full = (slice(0, rim), slice(rows - rim, rows), slice(rim, rows - rim))
     for j, part in enumerate(full):
+        if j == 2:
+            first.append((hi_w, lo_w, remote(10, ext.at[rows:rows + rim, mid], ext.at[0:rim, mid], up_w)))
+            first.append((lo_w, hi_w, remote(11, ext.at[rim:2 * rim, mid], ext.at[rows + rim:total, mid], dn_w)))
         there = slice(part.start + rim, part.stop + rim)
         first.append((hi_n, lo_n, remote(4 + 2 * j, ext.at[there, cols:cols + side], ext.at[there, ylo], up_n)))
         first.append((lo_n, hi_n, remote(5 + 2 * j, ext.at[there, side:2 * side], ext.at[there, yhi], dn_n)))
-    first.append((hi_w, lo_w, remote(10, ext.at[rows:rows + rim, mid], ext.at[0:rim, mid], up_w)))
-    first.append((lo_w, hi_w, remote(11, ext.at[rim:2 * rim, mid], ext.at[rows + rim:total, mid], dn_w)))
     local.wait()
     saves = []
 
@@ -121,7 +166,13 @@
             @pl.when(entry[0])
             def _(entry=entry):
                 entry[2].start()
-    for _g, comes, copy in later:
+        if k == 3:
+            @pl.when(later[0][1])
+            def _():
+                later[0][2].wait_recv()
+            fill_nodes(nodes, by_node, edges)
+            strain_pull(ns, nodes, pull)
+    for _g, comes, copy in later[1:]:
         @pl.when(comes)
         def _(copy=copy):
             copy.wait_recv()
@@ -141,22 +192,23 @@
         save.wait()
 
 
-def exchange(deformed, by_node, nw, nn):
+def exchange(deformed, by_node, ns, nw, nn):
     rows, cols, layers = deformed.shape
     rim = rows // 4 + 1
     shape = (rows + 2 * rim, cols + 2 * (rim - 1), layers)
     extra_in = jnp.stack([deformed[:, cols - rim], deformed[:, rim - 1]])
     anywhere = pl.BlockSpec(memory_space=pl.ANY)
     near = pl.BlockSpec(memory_space=pltpu.VMEM)
-    lanes = by_node.shape[-1]
+    nodes = jax.ShapeDtypeStruct((by_node.shape[0] + 1, QPAD, 128), F32)
     return pl.pallas_call(
-        functools.partial(halo_kernel, nw, nn, rim),
+        functools.partial(halo_kernel, nw, nn, rim, ns),
         out_shape=[jax.ShapeDtypeStruct(shape, BF16),
                    jax.ShapeDtypeStruct((2, rows + 2 * SIDE, layers), BF16),
-                   jax.ShapeDtypeStruct((3,) + by_node.shape[1:], F32)],
-        in_specs=[anywhere, near, near, near],
-        out_specs=[anywhere, near, near],
+                   nodes, nodes],
+        in_specs=[anywhere, near, near, near, near],
+        out_specs=[anywhere, near, near, near],
         scratch_shapes=[
+            pltpu.VMEM((3,) + by_node.shape[1:], F32),
             pltpu.VMEM(shape, BF16),
             pltpu.VMEM((shape[0], cols, layers), BF16),
             pltpu.SemaphoreType.DMA((21,)),
@@ -167,7 +219,7 @@
         compiler_params=pltpu.CompilerParams(
             collective_id=0, has_side_effects=True, vmem_limit_bytes=62 << 20),
         name="halo",
-    )(deformed, extra_in, by_node[0], by_node[:, 0])
+    )(deformed, extra_in, by_node[0], by_node[:, 0], by_node)
 
 
 def tables(rows, cols, layers, comps):
@@ -215,44 +267,10 @@
     return high, (value - high.astype(F32)).astype(BF16)
 
 
-def strain_pull(ns, nodes, pull):
-    npx = nodes.shape[0]
-    nel = npx - 1
-    lane = lax.broadcasted_iota(jnp.int32, (nel, 128), 1)
-    move = lambda a, by: pltpu.roll(a, by % 128, 1)
-    pull[...] = jnp.zeros_like(pull)
-
-    @pl.loop(0, nel)
-    def _(p):
-        a00, a01 = nodes[p, 0:nel], nodes[p, 1:nel + 1]
-        a10, a11 = nodes[p + 1, 0:nel], nodes[p + 1, 1:nel + 1]
-        dx = (a10 - a00) + (a11 - a01)
-        dy = (a01 - a00) + (a11 - a10)
-        every = (a00 + a01) + (a10 + a11)
-        slopes = (dx + move(dx, -1), dy + move(dy, -1), move(every, -1) - every)
-        f = [[0.03125 * (move(h, -ns * i) if i else h) + (1.0 if i == j else 0.0)
-              for j, h in enumerate(slopes)] for i in range(3)]
-        cof = [[f[(i + 1) % 3][(j + 1) % 3] * f[(i + 2) % 3][(j + 2) % 3]
-                - f[(i + 1) % 3][(j + 2) % 3] * f[(i + 2) % 3][(j + 1) % 3]
-                for j in range(3)] for i in range(3)]
-        ratio = f[0][0] * cof[0][0] + f[0][1] * cof[0][1] + f[0][2] * cof[0][2]
-        factor = (LAMBDA_BULK * jnp.log(ratio) - MU_SHEAR) / ratio
-        back = []
-        for j in range(3):
-            parts = [jnp.where(lane < ns - 1, MU_SHEAR * f[i][j] + factor * cof[i][j], 0.0) for i in range(3)]
-            back.append((parts[0] + move(parts[1], ns) + move(parts[2], 2 * ns)) * (0.03125 * REG_WEIGHT))
-        gx = back[0] + move(back[0], 1)
-        gy = back[1] + move(back[1], 1)
-        gz = move(back[2], 1) - back[2]
-        for dp, dq in ((0, 0), (0, 1), (1, 0), (1, 1)):
-            add = (gx if dp else -gx) + (gy if dq else -gy) + gz
-            pull[p + dp, dq:dq + nel] = pull[p + dp, dq:dq + nel] + add
-
-
-def tile_kernel(rim, ns, map_ref, ref_tile, ext, extra, by_node, edges,
+def tile_kernel(rim, map_ref, ref_tile, ext, extra, nodes, pull,
                 inter, proj, diag, up, down, down2, dz,
                 res, out,
-                rows_in, shift, samp, ndz, moved, gy, gz, sums, sq, gacc, dacc, nodes, pull, rimcol, sem):
+                rows_in, shift, samp, ndz, moved, gy, gz, sums, sq, gacc, dacc, rimcol, sem):
     p = pl.program_id(0)
     steps = pl.num_programs(0)
     cols, layers = samp.shape[1], samp.shape[2]
@@ -297,13 +315,6 @@
         gap = place - y - map_ref[1]
         shift[:cols] = jnp.where(gap == 0, 1.0, 0.0).astype(BF16)
         shift[cols:] = (jnp.where(gap == 1, 1.0, 0.0) - jnp.where(gap == -1, 1.0, 0.0)).astype(BF16)
-        nel = by_node.shape[0]
-        nodes[0:nel, 0:nel] = by_node[...]
-        nodes[nel, 0:nel] = edges[0]
-        top = lax.broadcasted_iota(jnp.int32, (QPAD - nel, 128), 0) == 0
-        for i in range(nel + 1):
-            row = edges[1, i:i + 1] if i < nel else edges[2, 0:1]
-            nodes[i, nel:QPAD] = jnp.where(top, jnp.broadcast_to(row, (QPAD - nel, 128)), 0.0)
         flat = nodes[...].reshape(-1, 128)
         high = flat.astype(BF16).astype(F32)
         both = jnp.concatenate([high, flat - high], axis=1).astype(BF16)
@@ -312,7 +323,6 @@
             part = level[i * QPAD:(i + 1) * QPAD]
             head = part.astype(BF16).astype(F32)
             ndz[i] = jnp.concatenate([head, part - head], axis=0).astype(BF16)
-        strain_pull(ns, nodes, pull)
         gacc[...] = jnp.zeros_like(gacc)
         dacc[...] = jnp.zeros_like(dacc)
         fetch(0, 2, steps).wait()
@@ -371,10 +381,10 @@
             out[k] = got + pull[...] if k == 0 else got
 
 
-def tile_terms(reference_tile, ext, extra, by_node, edges, offsets, ns):
+def tile_terms(reference_tile, ext, extra, nodes, pull, offsets):
     rows, cols, layers = reference_tile.shape
     comps = 3
-    npx = by_node.shape[0] + 1
+    npx = nodes.shape[0]
     rim = rows // 4 + 1
     tabs = tables(rows, cols, layers, comps)
     steps = rows // 8
@@ -385,7 +395,7 @@
     grid_spec = pltpu.PrefetchScalarGridSpec(
         num_scalar_prefetch=1,
         grid=(steps,),
-        in_specs=[slab, pl.BlockSpec(memory_space=pl.ANY), whole(extra), whole(by_node), whole(edges)]
+        in_specs=[slab, pl.BlockSpec(memory_space=pl.ANY), whole(extra), whole(nodes), whole(pull)]
         + [whole(t) for t in tabs],
         out_specs=[slab, whole(out_nodes)],
         scratch_shapes=[
@@ -400,20 +410,18 @@
             pltpu.VMEM((8 * cols, comps * layers), BF16),
             pltpu.VMEM((npx, QPAD, comps * layers), F32),
             pltpu.VMEM((npx, QPAD, comps * layers), F32),
-            pltpu.VMEM((npx, QPAD, 128), F32),
-            pltpu.VMEM((npx, QPAD, 128), F32),
             pltpu.VMEM(extra.shape, F32),
             pltpu.SemaphoreType.DMA((steps + 1,)),
         ],
     )
     return pl.pallas_call(
-        functools.partial(tile_kernel, rim, ns),
+        functools.partial(tile_kernel, rim),
         grid_spec=grid_spec,
         out_shape=[jax.ShapeDtypeStruct(reference_tile.shape, BF16), out_nodes],
         compiler_params=pltpu.CompilerParams(
             dimension_semantics=("arbitrary",), vmem_limit_bytes=62 << 20),
         name="tile",
-    )(offsets, reference_tile, ext, extra, by_node, edges, *tabs)
+    )(offsets, reference_tile, ext, extra, nodes, pull, *tabs)
 
 
 def node_kernel(nw, nn, terms, by_node, out, column, from_w, from_n, from_c, send, recv):
@@ -518,9 +526,9 @@
     comps, ns, nex, ney = displacement.shape
     by_node = displacement.transpose(2, 3, 0, 1).reshape(nex, ney, comps * ns)
     by_node = jnp.pad(by_node, ((0, 0), (0, 0), (0, 128 - comps * ns)))
-    ext, extra, edges = exchange(deformed_image, by_node, nw, nn)
+    ext, extra, nodes, pull = exchange(deformed_image, by_node, ns, nw, nn)
     residual, terms = tile_terms(
-        reference_image, ext, extra, by_node, edges, tile_map.reshape(2), ns)
+        reference_image, ext, extra, nodes, pull, tile_map.reshape(2))
     moved = node_update(terms, by_node, nw, nn)
     updated = moved[:, :, :comps * ns].reshape(nex, ney, comps, ns).transpose(2, 3, 0, 1)
     return (updated, residual)

time: 95.3 us -> 97.5 us (1.023)
  Pallas kernels: 87.2 us -> 89.5 us
    pallas_call x2, Pallas kernels: 78.7 us -> 80.5 us  [the longest x1 49.7 us: exchange(): pl.pallas_call(functools.partial(halo_kernel, nw, nn, rim, ns), out_shape...]
where the time goes in v3:
time: 97.5 us; the launch traced here: 97.3 us
  Pallas kernels  89.5 us (92%)
  local copies, waits for them, and re-layouts  6.43 us (7%)
    pallas_call x1, Pallas kernels, exchange(): pl.pallas_call(functools.partial(halo_kernel, nw, nn, rim, ns), out_shape...  49.7 us
    pallas_call x1, Pallas kernels, tile_terms(): pl.pallas_call(functools.partial(tile_kernel, rim), grid_spec=grid_spec,...  30.8 us
    pallas_call x1, Pallas kernels, node_update(): pl.pallas_call(functools.partial(node_kernel, nw, nn), out_shape=jax.Shap...  9.04 us

profile of v3, /device:TPU:12, one launch (start us, length us, event | category | flops | bytes accessed | tf_op | source)
XLA Modules:
  0.0 97.3 jit_solution(17200905694070757386)
XLA Ops:
  0.6 1.1 %fusion = (bf16[128,1,128]{2,1,0:T(2,128)(2,1)S(1)}, bf16[128,1,128]{2,1,0:T(2,128)(2,1)S(1)}) fusion(bf16[128,128,128]{2,1,0:T(8,128)(2,1)} %own.1), kind=kLoop, calls=%fused_computation.5 | loop fusion | bytes 131072 | tf_op jit(solution)/shard_map/slice | solution.py:199
  1.8 0.6 pad_maximum_fusion.extra_in
  2.4 1.3 %copy.19 = f32[16,16,3,17]{3,2,1,0:T(4,128)S(1)} copy(f32[16,16,3,17]{3,1,0,2:T(8,128)} %bitcast.13) | data formatting | bytes 104448 | tf_op jit(solution)/shard_map/transpose | solution.py:527
  3.7 0.2 reshape.14
  3.9 0.6 slice_bitcast_fusion.edge_x
  4.5 0.6 pad_slice_fusion
  5.1 0.7 pad.4.by_node
  5.8 49.7 %halo.1 = (bf16[194,192,128]{2,1,0:T(8,128)(2,1)}, bf16[2,224,128]{2,1,0:T(8,128)(2,1)}, f32[17,24,128]{2,1,0:T(8,128)}, f32[17,24,128]{2,1,0:T(8,128)}) custom-call(bf16[128,128,128]{2,1,0:T(8,128)(2,1)} %own.1, bf16[2,128,128]{2,1,0:T(8,128)(2,1)} %pad_maximum_fusion.extra_in, f32[16,128]{1,0:T(8,128)} %slice_bitcast_fusion.edge_x, f32[16,128]{1,0:T(8,128)} %bitcast.14, ...), custom_call_target="tpu_custom_call" | custom-call | tf_op jit(solution)/shard_map/halo/pallas_call | solution.py:203
  55.5 30.8 %tile.1 = (bf16[128,128,128]{2,1,0:T(8,128)(2,1)}, f32[2,17,24,128]{3,2,1,0:T(8,128)}) custom-call(s32[2]{0:T(128)} %bitcast.15, bf16[128,128,128]{2,1,0:T(8,128)(2,1)} %ref_tile.1, bf16[194,192,128]{2,1,0:T(8,128)(2,1)} %get-tuple-element.8.ext, bf16[2,224,128]{2,1,0:T(8,128)(2,1)} %get-tuple-element.9.extra, f32[17,24,128]{2,1,0:T(8,128)} %get-tuple-element.10.nodes, ...), custom_call_target="tpu_custom_call" | custom-call | tf_op jit(solution)/shard_map/tile/pallas_call | solution.py:417
  86.3 9.0 %nodes.1 = f32[16,16,128]{2,1,0:T(8,128)} custom-call(f32[2,17,24,128]{3,2,1,0:T(8,128)} %get-tuple-element.12.terms, f32[16,16,128]{2,1,0:T(8,128)} %pad.4.by_node), custom_call_target="tpu_custom_call" | custom-call | tf_op jit(solution)/shard_map/nodes/pallas_call | solution.py:507
  95.3 1.1 %reshape.15 = f32[16,16,3,17]{3,2,1,0:T(4,128)S(1)} reshape(f32[16,16,51]{2,1,0:T(8,128)} %bitcast.12) | data formatting | bytes 104448 | tf_op jit(solution)/shard_map/reshape | solution.py:533
  96.5 0.8 copy.20
  (1 shorter events, 0.0 us)
